TPU v7x, 128 devices: a whole 4x4x4 slice. The times are simulated.
128 devices in a mesh: space: 16 (over z_hi, x, core), chan: 8 (over y, z_lo).
Axes of the slice: x: 4, y: 4, z: 4 (z_hi: 2, z_lo: 2; z = z_hi * 2 + z_lo), core: 2. Of those that a mesh axis runs over, the one named last changes fastest.
Arguments:
- inputs: bfloat16 [128, 64, 32, 128], P('chan', 'space'), may hold values from -6 to 6
- filters: bfloat16 [27, 128, 128], P(None, 'chan'), may hold values from -0.109375 to 0.109375
- cotangent: bfloat16 [128, 64, 32, 128], P('chan', 'space'), may hold values from -6 to 6
Outputs:
- grad_inputs: bfloat16 [128, 64, 32, 128], P('chan', 'space')
- grad_filters: float32 [27, 128, 128], P(None, 'chan')
All inputs are finite; a program needn't handle non-finite values.
Results may differ from a plain program's by a relative error of at most 0.0049.
Values may be sent and summed in bfloat16 or wider, within the bound.
A program may use at most 128 MiB of HBM per device.

v0:
```python
import math
import jax
import jax.numpy as jnp
from jax import lax
from jax.sharding import PartitionSpec as P


def with_halo(block, sides, width):
    for axis, dim in sides:
        count = lax.axis_size(axis)
        forward = [(i, i + 1) for i in range(count - 1)]
        backward = [(target, source) for source, target in forward]
        low = lax.ppermute(
            lax.slice_in_dim(block, block.shape[dim] - width, None, axis=dim), axis, forward
        )
        high = lax.ppermute(lax.slice_in_dim(block, 0, width, axis=dim), axis, backward)
        block = jnp.concatenate([low, block, high], axis=dim)
    return block


def shifted(padded, depth_off, row_off, column_off, plane_count, row_count, column_count):
    return padded[
        :,
        depth_off : depth_off + plane_count,
        row_off : row_off + row_count,
        column_off : column_off + column_count,
    ]


def forward_part(padded, weights, plane_count, row_count, column_count):
    total = None
    for depth_off in range(3):
        stacked = jnp.concatenate(
            [
                shifted(
                    padded, depth_off, inner // 3, inner % 3, plane_count, row_count, column_count
                )
                for inner in range(9)
            ],
            axis=0,
        )
        block = weights[9 * depth_off : 9 * depth_off + 9].reshape(
            9 * weights.shape[1], weights.shape[2]
        )
        term = jnp.einsum("io,idhw->odhw", block, stacked, preferred_element_type=jnp.float32)
        total = term if total is None else total + term
    return total


def body(inputs, filters, cotangent):
    plane_count = inputs.shape[1]
    row_count = inputs.shape[2]
    column_count = inputs.shape[3]
    in_rim = with_halo(inputs, (("space", 1),), 1)
    in_pad = jnp.pad(in_rim, ((0, 0), (0, 0), (1, 1), (1, 1)))
    partial_sum = forward_part(in_pad, filters, plane_count, row_count, column_count)
    pre_act = lax.psum_scatter(partial_sum, "chan", scatter_dimension=0, tiled=True)
    sigma = jax.nn.sigmoid(pre_act)
    grad_out = (cotangent.astype(jnp.float32) * sigma * (1.0 + pre_act * (1.0 - sigma))).astype(
        jnp.bfloat16
    )
    grad_all = lax.all_gather(grad_out, "chan", axis=0, tiled=True)
    grad_rim = with_halo(grad_all, (("space", 1),), 1)
    grad_pad = jnp.pad(grad_rim, ((0, 0), (0, 0), (1, 1), (1, 1)))
    grad_in = None
    for offset in range(27):
        depth_off = offset // 9
        row_off = offset // 3 % 3
        column_off = offset % 3
        window = shifted(
            grad_pad,
            2 - depth_off,
            2 - row_off,
            2 - column_off,
            plane_count,
            row_count,
            column_count,
        )
        term = jnp.einsum(
            "io,odhw->idhw", filters[offset], window, preferred_element_type=jnp.float32
        )
        grad_in = term if grad_in is None else grad_in + term
    stacked_in = jnp.stack(
        [
            shifted(
                in_pad,
                offset // 9,
                offset // 3 % 3,
                offset % 3,
                plane_count,
                row_count,
                column_count,
            )
            for offset in range(27)
        ]
    )
    grad_w = jnp.einsum("kidhw,odhw->kio", stacked_in, grad_all, preferred_element_type=jnp.float32)
    grad_w = lax.psum(grad_w, "space")
    cell_total = plane_count * lax.axis_size("space") * row_count * column_count
    return (grad_in.astype(jnp.bfloat16), grad_w * (1.0 / math.sqrt(cell_total)))


def solution(mesh):
    placed = (P("chan", "space", None, None), P(None, "chan", None), P("chan", "space", None, None))
    return jax.shard_map(
        body,
        mesh=mesh,
        in_specs=placed,
        out_specs=(P("chan", "space", None, None), P(None, "chan", None)),
        check_vma=False,
    )
```

profile of v0, /device:TPU:7, one launch (start us, length us, event | category | flops | bytes accessed | tf_op | source)
XLA Modules:
  0.0 548.7 jit_solution(15890602798667119826)
XLA Ops:
  7.2 1.4 copy.42
  8.6 6.0 %collective-permute-start = (bf16[16,1,32,128]{3,0,2,1:T(8,128)(2,1)S(1)}, bf16[16,1,32,128]{3,0,2,1:T(8,128)(2,1)S(1)}, u32[]{:S(2)}, u32[]{:S(2)}) collective-permute-start(bf16[16,1,32,128]{3,0,2,1:T(8,128)(2,1)S(1)} %get-tuple-element.34), channel_id=1, source_target_pairs={{0,8},{8,16},{16,24},{24,32},{32,40},{40,48},{48,56},{56,64},{64,7... | collective-permute-start | bytes 393224 | tf_op jit(solution)/shard_map/ppermute | solution.py:13
  14.6 1.9 collective-permute-start.1
  17.4 7.1 %collective-permute-done.1 = bf16[16,1,32,128]{3,0,2,1:T(8,128)(2,1)S(1)} collective-permute-done((bf16[16,1,32,128]{3,0,2,1:T(8,128)(2,1)S(1)}, bf16[16,1,32,128]{3,0,2,1:T(8,128)(2,1)S(1)}, u32[]{:S(2)}, u32[]{:S(2)}) %collective-permute-start.1) | collective-permute-done | bytes 131104 | tf_op jit(solution)/shard_map/ppermute | solution.py:16
  24.5 1.1 select_maximum_fusion.2
  31.5 2.5 fusion.245
  34.0 2.5 fusion.246
  36.4 5.7 %add_bitcast_fusion = f32[128,4,32,128]{0,3,2,1:T(8,128)} fusion(f32[4,32,128,128]{3,2,1,0:T(8,128)S(1)} %fusion.245, f32[4,32,128,128]{3,2,1,0:T(8,128)S(1)} %fusion.246, bf16[144,4,32,128]{3,0,2,1:T(8,128)(2,1)S(1)} %get-tuple-element.8, bf16[144,128,1,1]{1,0,3,2:T(8,128)(2,1)S(1)} %bitcast.324), kind=kOutput, calls=%fused_computation.12 | convolution fusion | flops 608174080 | bytes 29921280 | tf_op jit(solution)/shard_map/io,idhw->odhw/dot_general | solution.py:45
  42.1 10.7 %copy.48 = f32[128,4,32,128]{3,2,1,0:T(8,128)} copy(f32[128,4,32,128]{0,3,2,1:T(8,128)} %add_bitcast_fusion) | data formatting | bytes 16777216 | tf_op jit(solution)/shard_map/add | solution.py:46
  52.9 167.8 %reduce-scatter.2.cloned.1.call-done = f32[16,4,32,128]{3,2,1,0:T(8,128)} async-done(((f32[128,4,32,128]{3,2,1,0:T(8,128)}), f32[16,4,32,128]{3,2,1,0:T(8,128)}) %reduce-scatter.2.cloned.1.call-update) | async-done | bytes 1048592 | tf_op jit(solution)/shard_map/reduce_scatter | solution.py:57
  220.7 2.4 multiply_convert_fusion
  235.7 1.1 bitcast_dynamic-update-slice_fusion.13
  238.8 1.1 bitcast_dynamic-update-slice_fusion.10
  241.8 1.0 bitcast_dynamic-update-slice_fusion.7
  249.5 63.8 %all-gather.2.cloned.1.call-done = bf16[128,4,32,128]{3,2,1,0:T(8,128)(2,1)} async-done(((bf16[16,4,32,128]{3,2,1,0:T(8,128)(2,1)}), bf16[128,4,32,128]{3,2,1,0:T(8,128)(2,1)}) %all-gather.2.cloned.1.call-update) | async-done | bytes 4194320 | tf_op jit(solution)/shard_map/all_gather | solution.py:62
  313.3 5.0 copy.49
  318.4 2.0 copy-done
  320.4 1.1 fusion.242
  321.6 3.3 collective-permute-start.3
  324.8 5.9 %collective-permute-start.2 = (bf16[128,1,32,128]{3,0,2,1:T(8,128)(2,1)S(1)}, bf16[128,1,32,128]{3,0,2,1:T(8,128)(2,1)S(1)}, u32[]{:S(2)}, u32[]{:S(2)}) collective-permute-start(bf16[128,1,32,128]{3,0,2,1:T(8,128)(2,1)S(1)} %get-tuple-element.6), channel_id=1, source_target_pairs={{0,8},{8,16},{16,24},{24,32},{32,40},{40,48},{48,56},{56,64},{64,7... | collective-permute-start | bytes 3145736 | tf_op jit(solution)/shard_map/ppermute | solution.py:13
  330.8 7.9 %fusion.179 = f32[27,16,128]{2,1,0:T(8,128)} fusion(bf16[27,16,4,32,128]{4,1,3,2,0:T(8,128)(2,1)} %bitcast_dynamic-update-slice_fusion, bf16[128,4,32,128,1]{3,2,1,0,4:T(8,128)(2,1)S(1)} %bitcast.323), kind=kOutput, calls=%fused_computation.120 | convolution fusion | flops 1811939328 | bytes 18571264 | tf_op jit(solution)/shard_map/kidhw,odhw->kio/dot_general | solution.py:97
  338.6 5.5 %fusion.197 = f32[4,32,128,16]{2,3,1,0:T(8,128)} fusion(bf16[27,16,128]{2,1,0:T(8,128)(2,1)S(1)} %copy-done.11, bf16[128,4,32,128]{3,2,1,0:T(8,128)(2,1)} %all-gather.2.cloned.1.call-done), kind=kOutput, calls=%fused_computation.192 | convolution fusion | flops 67108864 | bytes 5246976 | tf_op jit(solution)/shard_map/io,odhw->idhw/dot_general | solution.py:79
  344.1 131.4 %all-reduce.4.cloned.1.call-done = f32[27,16,128]{2,1,0:T(8,128)} async-done(((f32[27,16,128]{2,1,0:T(8,128)}), f32[27,16,128]{2,1,0:T(8,128)}) %all-reduce.4.cloned.1.call-update) | async-done | bytes 221200 | tf_op jit(solution)/shard_map/psum | solution.py:98
  475.5 1.6 broadcast_multiply_fusion
  477.1 9.9 %select_maximum_fusion = bf16[128,6,34,130]{3,0,2,1:T(8,128)(2,1)S(1)} fusion(bf16[128,1,32,128]{3,0,2,1:T(8,128)(2,1)S(1)} %collective-permute-done.3, bf16[128,4,32,128]{3,0,2,1:T(8,128)(2,1)} %copy-done, bf16[128,1,32,128]{3,0,2,1:T(8,128)(2,1)S(1)} %collective-permute-done.2), kind=kLoop, calls=%fused_computation.7 | loop fusion | flops 64496640 | bytes 13080576 | tf_op jit(solution)/shard_map/concatenate | solution.py:17
  487.0 1.5 fusion.32
  488.5 1.6 fusion.34
  490.2 2.6 fusion.36
  492.7 2.5 fusion.38
  495.3 1.7 fusion.40
  497.0 2.5 fusion.42
  499.5 2.5 fusion.44
  502.0 1.7 fusion.46
  503.6 2.5 fusion.50
  506.1 1.7 fusion.52
  507.8 2.7 fusion.54
  510.5 1.5 fusion.26
  512.0 1.5 fusion.28
  514.2 1.5 fusion.76
  515.7 1.5 fusion.79
  517.9 2.5 fusion.85
  520.4 1.7 fusion.89
  522.1 2.5 fusion.92
  524.6 2.8 fusion.95
  527.3 1.6 fusion.98
  529.0 1.6 fusion.48
  530.6 6.3 %fusion.173 = f32[4,32,128,16]{2,3,1,0:T(8,128)S(1)} fusion(f32[4,32,128,16]{2,3,1,0:T(8,128)S(1)} %copy-done.4, f32[4,32,128,16]{2,3,1,0:T(8,128)S(1)} %fusion.32, f32[4,32,128,16]{2,3,1,0:T(8,128)} %fusion.34, f32[4,32,128,16]{2,3,1,0:T(8,128)} %fusion.36, f32[4,32,128,16]{2,3,1,0:T(8,128)} %fusion.38, f32[4,32,128,16]{2,3,1,0:T(8,128)} %fusion.40, ...), kind=kOutput, calls=%fused_computation.118 | convolution fusion | flops 70516736 | bytes 18878464 | tf_op jit(solution)/shard_map/io,odhw->idhw/dot_general | solution.py:79
  539.4 1.4 fusion.176
  (71 shorter events, 34.7 us)
Async XLA Ops:
  7.2 213.5 %reduce-scatter.2.cloned.1.call-start = ((), (), s32[]{:S(2)}) async-start(), calls=%async_computation.1 | async-start | bytes 9437184 | tf_op jit(solution)/shard_map/reduce_scatter | solution.py:57
  8.6 8.7 %collective-permute-start = (bf16[16,1,32,128]{3,0,2,1:T(8,128)(2,1)S(1)}, bf16[16,1,32,128]{3,0,2,1:T(8,128)(2,1)S(1)}, u32[]{:S(2)}, u32[]{:S(2)}) collective-permute-start(bf16[16,1,32,128]{3,0,2,1:T(8,128)(2,1)S(1)} %get-tuple-element.34), channel_id=1, source_target_pairs={{0,8},{8,16},{16,24},{24,32},{32,40},{40,48},{48,56},{56,64},{64,7... | collective-permute-start | bytes 393224 | tf_op jit(solution)/shard_map/ppermute | solution.py:13
  14.6 9.9 %collective-permute-start.1 = (bf16[16,1,32,128]{3,0,2,1:T(8,128)(2,1)S(1)}, bf16[16,1,32,128]{3,0,2,1:T(8,128)(2,1)S(1)}, u32[]{:S(2)}, u32[]{:S(2)}) collective-permute-start(bf16[16,1,32,128]{3,0,2,1:T(8,128)(2,1)S(1)} %get-tuple-element.35), channel_id=1, source_target_pairs={{8,0},{16,8},{24,16},{32,24},{40,32},{48,40},{56,48},{64,56},{72,6... | collective-permute-start | bytes 393224 | tf_op jit(solution)/shard_map/ppermute | solution.py:16
  25.8 2.0 copy-start.3
  52.8 167.9 %copy-start.10 = (bf16[16,4,32,128]{3,2,1,0:T(8,128)(2,1)S(1)}, bf16[16,4,32,128]{3,2,1,0:T(8,128)(2,1)}, u32[]{:S(2)}) copy-start(bf16[16,4,32,128]{3,2,1,0:T(8,128)(2,1)} %param.5) | copy-start | bytes 1572868
  52.8 260.5 %all-gather.2.cloned.1.call-start = ((), (), s32[]{:S(2)}) async-start(), calls=%async_computation.2 | async-start | bytes 4718592 | tf_op jit(solution)/shard_map/all_gather | solution.py:62
  223.1 252.4 %all-reduce.4.cloned.1.call-start = ((), (), s32[]{:S(2)}) async-start(), calls=%async_computation.3 | async-start | bytes 442368 | tf_op jit(solution)/shard_map/psum | solution.py:98
  313.3 17.4 %copy-start.2 = (bf16[128,4,32,128]{3,2,1,0:T(8,128)(2,1)S(1)}, bf16[128,4,32,128]{3,2,1,0:T(8,128)(2,1)}, u32[]{:S(2)}) copy-start(bf16[128,4,32,128]{3,2,1,0:T(8,128)(2,1)} %all-gather.2.cloned.1.call-done) | copy-start | bytes 12582916
  318.4 2.0 copy-start
  321.6 155.6 %collective-permute-start.3 = (bf16[128,1,32,128]{3,0,2,1:T(8,128)(2,1)}, bf16[128,1,32,128]{3,0,2,1:T(8,128)(2,1)S(1)}, u32[]{:S(2)}, u32[]{:S(2)}) collective-permute-start(bf16[128,1,32,128]{3,0,2,1:T(8,128)(2,1)} %get-tuple-element.7), channel_id=1, source_target_pairs={{8,0},{16,8},{24,16},{32,24},{40,32},{48,40},{56,48},{64,56},{72,6... | collective-permute-start | bytes 3145736 | tf_op jit(solution)/shard_map/ppermute | solution.py:16
  324.8 152.3 %collective-permute-start.2 = (bf16[128,1,32,128]{3,0,2,1:T(8,128)(2,1)S(1)}, bf16[128,1,32,128]{3,0,2,1:T(8,128)(2,1)S(1)}, u32[]{:S(2)}, u32[]{:S(2)}) collective-permute-start(bf16[128,1,32,128]{3,0,2,1:T(8,128)(2,1)S(1)} %get-tuple-element.6), channel_id=1, source_target_pairs={{0,8},{8,16},{16,24},{24,32},{32,40},{40,48},{48,56},{56,64},{64,7... | collective-permute-start | bytes 3145736 | tf_op jit(solution)/shard_map/ppermute | solution.py:13
  330.7 7.9 %copy-start.11 = (bf16[27,16,128]{2,1,0:T(8,128)(2,1)S(1)}, bf16[27,16,128]{2,1,0:T(8,128)(2,1)}, u32[]{:S(2)}) copy-start(bf16[27,16,128]{2,1,0:T(8,128)(2,1)} %param.4) | copy-start | bytes 331780
  524.6 4.4 copy-start.1
  527.3 3.3 copy-start.4
  536.9 1.2 copy-start.5
  536.9 1.5 copy-start.6
  536.9 1.8 copy-start.7
  536.9 2.1 copy-start.8
  537.0 2.5 copy-start.9
Sparse Core Ops, SparseCore 0:
  52.9 167.6 reduce-scatter.1
  223.3 90.0 all-gather.1
  338.8 136.7 all-reduce.3
where the time goes:
time: 558 us; the launch traced here: 549 us
  waiting for transfers between devices  370 us (66%)
  matrix products  75.9 us (14%)
  local copies, waits for them, and re-layouts  53.7 us (10%)
  other arithmetic  17.3 us (3%)
  starting transfers between devices  17.2 us (3%)
  between operations  14.5 us (3%)
    reduce_scatter x1, waiting for transfers between devices, body(): lax.psum_scatter(partial_sum, 'chan', scatter_dimension=0, tiled=True)  168 us
    psum x1, waiting for transfers between devices, body(): grad_w = lax.psum(grad_w, 'space')  131 us
    all_gather x1, waiting for transfers between devices, body(): grad_all = lax.all_gather(grad_out, 'chan', axis=0, tiled=True)  63.8 us
    dot_general x27, matrix products, body(): jnp.einsum('io,odhw->idhw', filters[offset], window, preferred_element_ty...  57.4 us
    unnamed x57, local copies, waits for them, and re-layouts  34.1 us
    ppermute x2, starting transfers between devices, with_halo(): lax.ppermute(lax.slice_in_dim(block, block.shape[dim] - width, None, axis...  11.9 us
  transfers between devices with their start and end apart: 7, of which 4 were waited for; matrix products, arithmetic and copies ran while one was open for 8% of the time, Pallas kernels for 0%

commit v1 on v0

--- a/solution.py
+++ b/solution.py
@@ -59,7 +59,9 @@
     grad_out = (cotangent.astype(jnp.float32) * sigma * (1.0 + pre_act * (1.0 - sigma))).astype(
         jnp.bfloat16
     )
-    grad_all = lax.all_gather(grad_out, "chan", axis=0, tiled=True)
+    grad_all = jnp.concatenate(
+        lax.all_to_all(jnp.stack([grad_out] * lax.axis_size("chan")), "chan", 0, 0), axis=0
+    )
     grad_rim = with_halo(grad_all, (("space", 1),), 1)
     grad_pad = jnp.pad(grad_rim, ((0, 0), (0, 0), (1, 1), (1, 1)))
     grad_in = None

time: 558 us -> 528 us (0.946)
  waiting for transfers between devices: 370 us -> 338 us
    all_gather x1 -> x0, waiting for transfers between devices: 63.8 us -> none  [body(): grad_all = lax.all_gather(grad_out, 'chan', axis=0, tiled=True)]
    all_to_all x0 -> x1, waiting for transfers between devices: none -> 43.2 us  [body(): lax.all_to_all(jnp.stack([grad_out] * lax.axis_size('chan')), 'chan', 0, 0)]
    reduce_scatter x1, waiting for transfers between devices: 168 us -> 157 us  [body(): lax.psum_scatter(partial_sum, 'chan', scatter_dimension=0, tiled=True)]
    unnamed x57 -> x55, local copies, waits for them, and re-layouts: 34.1 us -> 32 us
where the time goes in v1:
time: 528 us; the launch traced here: 518 us
  waiting for transfers between devices  338 us (64%)
  matrix products  74.2 us (14%)
  local copies, waits for them, and re-layouts  53.4 us (10%)
  starting transfers between devices  21.7 us (4%)
  other arithmetic  16.5 us (3%)
  between operations  14.5 us (3%)
    reduce_scatter x1, waiting for transfers between devices, body(): lax.psum_scatter(partial_sum, 'chan', scatter_dimension=0, tiled=True)  157 us
    psum x1, waiting for transfers between devices, body(): grad_w = lax.psum(grad_w, 'space')  130 us
    dot_general x27, matrix products, body(): jnp.einsum('io,odhw->idhw', filters[offset], window, preferred_element_ty...  55.8 us
    all_to_all x1, waiting for transfers between devices, body(): lax.all_to_all(jnp.stack([grad_out] * lax.axis_size('chan')), 'chan', 0, 0)  43.2 us
    unnamed x55, local copies, waits for them, and re-layouts  32 us
    ppermute x2, starting transfers between devices, with_halo(): lax.ppermute(lax.slice_in_dim(block, block.shape[dim] - width, None, axis...  11.8 us
    concatenate x2, other arithmetic, with_halo(): block = jnp.concatenate([low, block, high], axis=dim)  11 us
    dot_general x3, matrix products, forward_part(): jnp.einsum('io,idhw->odhw', block, stacked, preferred_element_type=jnp.fl...  10.6 us
  transfers between devices with their start and end apart: 7, of which 4 were waited for; matrix products, arithmetic and copies ran while one was open for 8% of the time, Pallas kernels for 0%

profile of v1, /device:TPU:7, one launch (start us, length us, event | category | flops | bytes accessed | tf_op | source)
XLA Modules:
  0.0 518.0 jit_solution(7903634146987105464)
XLA Ops:
  7.2 1.4 copy.15
  8.6 6.0 %collective-permute-start = (bf16[16,1,32,128]{3,0,2,1:T(8,128)(2,1)S(1)}, bf16[16,1,32,128]{3,0,2,1:T(8,128)(2,1)S(1)}, u32[]{:S(2)}, u32[]{:S(2)}) collective-permute-start(bf16[16,1,32,128]{3,0,2,1:T(8,128)(2,1)S(1)} %get-tuple-element.34), channel_id=1, source_target_pairs={{0,8},{8,16},{16,24},{24,32},{32,40},{40,48},{48,56},{56,64},{64,7... | collective-permute-start | bytes 393224 | tf_op jit(solution)/shard_map/ppermute | solution.py:13
  14.6 1.9 collective-permute-start.1
  17.4 7.1 %collective-permute-done.1 = bf16[16,1,32,128]{3,0,2,1:T(8,128)(2,1)S(1)} collective-permute-done((bf16[16,1,32,128]{3,0,2,1:T(8,128)(2,1)S(1)}, bf16[16,1,32,128]{3,0,2,1:T(8,128)(2,1)S(1)}, u32[]{:S(2)}, u32[]{:S(2)}) %collective-permute-start.1) | collective-permute-done | bytes 131104 | tf_op jit(solution)/shard_map/ppermute | solution.py:16
  24.5 1.1 select_maximum_fusion.2
  31.5 2.5 fusion.238
  34.0 2.5 fusion.239
  36.4 5.7 %add_bitcast_fusion = f32[128,4,32,128]{0,3,2,1:T(8,128)} fusion(f32[4,32,128,128]{3,2,1,0:T(8,128)S(1)} %fusion.238, f32[4,32,128,128]{3,2,1,0:T(8,128)S(1)} %fusion.239, bf16[144,4,32,128]{3,0,2,1:T(8,128)(2,1)S(1)} %get-tuple-element.8, bf16[144,128,1,1]{1,0,3,2:T(8,128)(2,1)S(1)} %bitcast.332), kind=kOutput, calls=%fused_computation.12 | convolution fusion | flops 608174080 | bytes 29921280 | tf_op jit(solution)/shard_map/io,idhw->odhw/dot_general | solution.py:45
  42.2 10.5 %copy.21 = f32[128,4,32,128]{3,2,1,0:T(8,128)} copy(f32[128,4,32,128]{0,3,2,1:T(8,128)} %add_bitcast_fusion) | data formatting | bytes 16777216 | tf_op jit(solution)/shard_map/add | solution.py:46
  63.2 157.3 %reduce-scatter.2.cloned.1.call-done = f32[16,4,32,128]{3,2,1,0:T(8,128)} async-done(((f32[128,4,32,128]{3,2,1,0:T(8,128)}), f32[16,4,32,128]{3,2,1,0:T(8,128)}) %reduce-scatter.2.cloned.1.call-update) | async-done | bytes 1048592 | tf_op jit(solution)/shard_map/reduce_scatter | solution.py:57
  220.6 1.6 multiply_convert_fusion
  222.6 3.0 stack.95
  225.6 4.6 all-to-all-start
  232.1 1.1 bitcast_dynamic-update-slice_fusion.13
  235.2 1.1 bitcast_dynamic-update-slice_fusion.10
  246.0 43.2 %all-to-all-done = bf16[8,16,4,32,128]{4,1,3,2,0:T(8,128)(2,1)} async-done(((bf16[8,16,4,32,128]{4,1,3,2,0:T(8,128)(2,1)}), bf16[8,16,4,32,128]{4,1,3,2,0:T(8,128)(2,1)}, u32[]{:S(2)}, u32[]{:S(2)}) %all-to-all-start) | async-done | bytes 4194336 | tf_op jit(solution)/shard_map/all_to_all | solution.py:63
  289.2 3.4 copy.23
  292.6 1.3 fusion.235
  293.9 3.4 collective-permute-start.3
  297.3 5.8 %collective-permute-start.2 = (bf16[128,1,32,128]{3,0,2,1:T(8,128)(2,1)S(1)}, bf16[128,1,32,128]{3,0,2,1:T(8,128)(2,1)S(1)}, u32[]{:S(2)}, u32[]{:S(2)}) collective-permute-start(bf16[128,1,32,128]{3,0,2,1:T(8,128)(2,1)S(1)} %get-tuple-element.6), channel_id=1, source_target_pairs={{0,8},{8,16},{16,24},{24,32},{32,40},{40,48},{48,56},{56,64},{64,7... | collective-permute-start | bytes 3145736 | tf_op jit(solution)/shard_map/ppermute | solution.py:13
  303.1 7.7 %convolution_bitcast_fusion = f32[27,16,128]{2,1,0:T(8,128)} fusion(bf16[27,16,4,32,128]{4,1,3,2,0:T(8,128)(2,1)} %bitcast_dynamic-update-slice_fusion, bf16[128,4,32,128,1]{3,0,2,1,4:T(8,128)(2,1)S(1)} %bitcast.327), kind=kOutput, calls=%fused_computation.117 | convolution fusion | flops 1811939328 | bytes 18571264 | tf_op jit(solution)/shard_map/kidhw,odhw->kio/dot_general | solution.py:99
  310.9 3.8 fusion.191
  314.7 129.9 %all-reduce.4.cloned.1.call-done = f32[27,16,128]{2,1,0:T(8,128)} async-done(((f32[27,16,128]{2,1,0:T(8,128)}), f32[27,16,128]{2,1,0:T(8,128)}) %all-reduce.4.cloned.1.call-update) | async-done | bytes 221200 | tf_op jit(solution)/shard_map/psum | solution.py:100
  444.7 1.6 broadcast_multiply_fusion
  446.3 9.9 %select_maximum_fusion = bf16[128,6,34,130]{3,0,2,1:T(8,128)(2,1)S(1)} fusion(bf16[128,1,32,128]{3,0,2,1:T(8,128)(2,1)S(1)} %collective-permute-done.3, bf16[128,4,32,128]{3,0,2,1:T(8,128)(2,1)} %bitcast.329, bf16[128,1,32,128]{3,0,2,1:T(8,128)(2,1)S(1)} %collective-permute-done.2), kind=kLoop, calls=%fused_computation.7 | loop fusion | flops 64496640 | bytes 13080576 | tf_op jit(solution)/shard_map/concatenate | solution.py:17
  456.2 1.5 fusion.32
  457.7 1.6 fusion.34
  459.3 2.6 fusion.36
  461.9 2.6 fusion.38
  464.5 1.7 fusion.40
  466.2 2.5 fusion.42
  468.7 2.5 fusion.44
  471.2 1.7 fusion.46
  472.8 2.5 fusion.50
  475.4 1.6 fusion.52
  477.0 2.9 fusion.54
  479.9 1.5 fusion.26
  481.4 1.5 fusion.28
  483.6 1.5 fusion.73
  485.1 1.5 fusion.76
  487.3 2.5 fusion.82
  489.8 1.7 fusion.86
  491.5 2.5 fusion.89
  493.9 2.7 fusion.92
  496.6 1.6 fusion.95
  498.2 1.6 fusion.48
  499.9 6.3 %fusion.170 = f32[4,32,128,16]{2,3,1,0:T(8,128)S(1)} fusion(f32[4,32,128,16]{2,3,1,0:T(8,128)S(1)} %copy-done.3, f32[4,32,128,16]{2,3,1,0:T(8,128)S(1)} %fusion.32, f32[4,32,128,16]{2,3,1,0:T(8,128)} %fusion.34, f32[4,32,128,16]{2,3,1,0:T(8,128)} %fusion.36, f32[4,32,128,16]{2,3,1,0:T(8,128)} %fusion.38, f32[4,32,128,16]{2,3,1,0:T(8,128)} %fusion.40, ...), kind=kOutput, calls=%fused_computation.115 | convolution fusion | flops 70516736 | bytes 18878464 | tf_op jit(solution)/shard_map/io,odhw->idhw/dot_general | solution.py:81
  508.7 1.4 fusion.173
  (70 shorter events, 35.9 us)
Async XLA Ops:
  7.2 213.4 %reduce-scatter.2.cloned.1.call-start = ((), (), s32[]{:S(2)}) async-start(), calls=%async_computation.2 | async-start | bytes 9437184 | tf_op jit(solution)/shard_map/reduce_scatter | solution.py:57
  8.6 8.7 %collective-permute-start = (bf16[16,1,32,128]{3,0,2,1:T(8,128)(2,1)S(1)}, bf16[16,1,32,128]{3,0,2,1:T(8,128)(2,1)S(1)}, u32[]{:S(2)}, u32[]{:S(2)}) collective-permute-start(bf16[16,1,32,128]{3,0,2,1:T(8,128)(2,1)S(1)} %get-tuple-element.34), channel_id=1, source_target_pairs={{0,8},{8,16},{16,24},{24,32},{32,40},{40,48},{48,56},{56,64},{64,7... | collective-permute-start | bytes 393224 | tf_op jit(solution)/shard_map/ppermute | solution.py:13
  14.6 9.9 %collective-permute-start.1 = (bf16[16,1,32,128]{3,0,2,1:T(8,128)(2,1)S(1)}, bf16[16,1,32,128]{3,0,2,1:T(8,128)(2,1)S(1)}, u32[]{:S(2)}, u32[]{:S(2)}) collective-permute-start(bf16[16,1,32,128]{3,0,2,1:T(8,128)(2,1)S(1)} %get-tuple-element.35), channel_id=1, source_target_pairs={{8,0},{16,8},{24,16},{32,24},{40,32},{48,40},{56,48},{64,56},{72,6... | collective-permute-start | bytes 393224 | tf_op jit(solution)/shard_map/ppermute | solution.py:16
  25.8 2.0 copy-start.2
  54.6 165.9 %copy-start.9 = (bf16[16,4,32,128]{3,2,1,0:T(8,128)(2,1)S(1)}, bf16[16,4,32,128]{3,2,1,0:T(8,128)(2,1)}, u32[]{:S(2)}) copy-start(bf16[16,4,32,128]{3,2,1,0:T(8,128)(2,1)} %param.5) | copy-start | bytes 1572868
  225.6 63.6 %all-to-all-start = ((bf16[8,16,4,32,128]{4,1,3,2,0:T(8,128)(2,1)}), bf16[8,16,4,32,128]{4,1,3,2,0:T(8,128)(2,1)}, u32[]{:S(2)}, u32[]{:S(2)}) async-start(bf16[8,16,4,32,128]{4,1,3,2,0:T(8,128)(2,1)} %stack.95), calls=%async_computation.1 | async-start | bytes 8388608 | tf_op jit(solution)/shard_map/all_to_all | solution.py:63
  230.1 214.5 %all-reduce.4.cloned.1.call-start = ((), (), s32[]{:S(2)}) async-start(), calls=%async_computation.3 | async-start | bytes 442368 | tf_op jit(solution)/shard_map/psum | solution.py:100
  292.6 10.5 %copy-start = (bf16[8,16,4,32,128]{4,1,0,3,2:T(8,128)(2,1)}, bf16[8,16,4,32,128]{4,1,0,3,2:T(8,128)(2,1)S(1)}, u32[]{:S(2)}) copy-start(bf16[8,16,4,32,128]{4,1,0,3,2:T(8,128)(2,1)S(1)} %copy.23) | copy-start | bytes 12582916
  293.9 152.4 %collective-permute-start.3 = (bf16[128,1,32,128]{3,0,2,1:T(8,128)(2,1)}, bf16[128,1,32,128]{3,0,2,1:T(8,128)(2,1)S(1)}, u32[]{:S(2)}, u32[]{:S(2)}) collective-permute-start(bf16[128,1,32,128]{3,0,2,1:T(8,128)(2,1)} %get-tuple-element.7), channel_id=1, source_target_pairs={{8,0},{16,8},{24,16},{32,24},{40,32},{48,40},{56,48},{64,56},{72,6... | collective-permute-start | bytes 3145736 | tf_op jit(solution)/shard_map/ppermute | solution.py:16
  297.3 149.0 %collective-permute-start.2 = (bf16[128,1,32,128]{3,0,2,1:T(8,128)(2,1)S(1)}, bf16[128,1,32,128]{3,0,2,1:T(8,128)(2,1)S(1)}, u32[]{:S(2)}, u32[]{:S(2)}) collective-permute-start(bf16[128,1,32,128]{3,0,2,1:T(8,128)(2,1)S(1)} %get-tuple-element.6), channel_id=1, source_target_pairs={{0,8},{8,16},{16,24},{24,32},{32,40},{40,48},{48,56},{56,64},{64,7... | collective-permute-start | bytes 3145736 | tf_op jit(solution)/shard_map/ppermute | solution.py:13
  303.1 7.8 %copy-start.10 = (bf16[27,16,128]{2,1,0:T(8,128)(2,1)S(1)}, bf16[27,16,128]{2,1,0:T(8,128)(2,1)}, u32[]{:S(2)}) copy-start(bf16[27,16,128]{2,1,0:T(8,128)(2,1)} %param.4) | copy-start | bytes 331780
  493.9 4.3 copy-start.1
  496.6 3.3 copy-start.3
  506.2 1.2 copy-start.4
  506.2 1.5 copy-start.5
  506.2 1.8 copy-start.6
  506.2 2.1 copy-start.7
  506.2 2.5 copy-start.8
Sparse Core Ops, SparseCore 0:
  52.8 167.6 reduce-scatter.1
  311.0 133.6 all-reduce.3
